TPU v7x, 32 devices: a whole 2x2x4 slice. The times are simulated.
32 devices in a mesh: dp: 8 (over y, x, core), tensor: 4 (over z).
Axes of the slice: x: 2, y: 2, z: 4, core: 2. Of those that a mesh axis runs over, the one named last changes fastest.
Arguments:
- inputs: bfloat16 [2048, 2048], P(('dp', 'tensor')), parts along dimension 0, may hold values from -6 to 6
- grad_out: bfloat16 [2048, 2048], P(('dp', 'tensor')), parts along dimension 0, may hold values from -6 to 6
- gate_weight: bfloat16 [2048, 7168], P(None, 'tensor'), may hold values from -6 to 6
- up_weight: bfloat16 [2048, 7168], P(None, 'tensor'), may hold values from -6 to 6
- down_weight: bfloat16 [7168, 2048], P('tensor'), may hold values from -6 to 6
Outputs:
- grad_inputs: bfloat16 [2048, 2048], P(('dp', 'tensor')), parts along dimension 0
- grad_gate: bfloat16 [16384, 7168], P('dp', 'tensor'), parts along dimension 0
- grad_up: bfloat16 [16384, 7168], P('dp', 'tensor'), parts along dimension 0
- grad_down: bfloat16 [57344, 2048], P(('dp', 'tensor')), parts along dimension 0
There are 8 independent parts, one for each index of `dp`. A program takes and returns all parts, laid end to end along the dimension named above; an argument that names none is the same for every part. Nothing has to cross between parts.
All inputs are finite; a program needn't handle non-finite values.
Results may differ from a plain program's by a relative error of at most 0.0049.
Values may be sent and summed in bfloat16 or wider, within the bound.
A program may use at most 128 MiB of HBM per device.

v0:
```python
import jax
import jax.numpy as jnp
from jax import lax
from jax.sharding import PartitionSpec as P

D = 2048
FF = 7168


def contract_last(left, right):
    return lax.dot_general(
        left, right, (((1,), (1,)), ((), ())), preferred_element_type=jnp.float32
    )


def contract_first(left, right):
    return lax.dot_general(
        left, right, (((0,), (0,)), ((), ())), preferred_element_type=jnp.float32
    )


def on_device(inputs, grad_out, gate_weight, up_weight, down_weight):
    tokens_all = lax.all_gather(inputs, "tensor", axis=0, tiled=True)
    grads_all = lax.all_gather(grad_out, "tensor", axis=0, tiled=True)
    inv_width = D ** (-0.5)
    inv_rows = tokens_all.shape[0] ** (-0.5)
    inv_hidden = (2 * FF) ** (-0.5)
    gate = jnp.dot(tokens_all, gate_weight, preferred_element_type=jnp.float32) * inv_width
    up = jnp.dot(tokens_all, up_weight, preferred_element_type=jnp.float32) * inv_width
    sig = jax.nn.sigmoid(gate)
    act = gate * sig
    hidden = (act * up).astype(jnp.bfloat16)
    d_hidden = contract_last(grads_all, down_weight) * inv_width
    grad_down = (contract_first(hidden, grads_all) * inv_rows).astype(jnp.bfloat16)
    d_gate = (d_hidden * up * sig * (1.0 + gate * (1.0 - sig))).astype(jnp.bfloat16)
    d_up = (d_hidden * act).astype(jnp.bfloat16)
    grad_gate = (contract_first(tokens_all, d_gate) * inv_rows).astype(jnp.bfloat16)
    grad_up = (contract_first(tokens_all, d_up) * inv_rows).astype(jnp.bfloat16)
    summed = lax.psum_scatter(
        contract_last(d_gate, gate_weight) * inv_hidden
        + contract_last(d_up, up_weight) * inv_hidden,
        "tensor",
        scatter_dimension=0,
        tiled=True,
    )
    grad_inputs = summed.astype(jnp.bfloat16)
    return (grad_inputs, grad_gate, grad_up, grad_down)


def solution(mesh):
    placed = (
        P(("dp", "tensor"), None),
        P(("dp", "tensor"), None),
        P(None, "tensor"),
        P(None, "tensor"),
        P("tensor", None),
    )
    return jax.shard_map(
        on_device,
        mesh=mesh,
        in_specs=placed,
        out_specs=(
            P(("dp", "tensor"), None),
            P("dp", "tensor"),
            P("dp", "tensor"),
            P(("dp", "tensor"), None),
        ),
        check_vma=False,
    )
```

profile of v0, /device:TPU:0, one launch (start us, length us, event | category | flops | bytes accessed | tf_op | source)
XLA Modules:
  0.0 139.9 jit_solution(8619819542554499196)
XLA Ops:
  7.2 0.0 all-gather.5.cloned.1.call-start
  7.2 0.7 all-gather.5.cloned.1.call-update
  7.9 0.0 all-gather.3.cloned.1.call-start
  7.9 0.7 all-gather.3.cloned.1.call-update
  8.6 0.0 reduce-scatter.2.cloned.1.call-start
  8.7 31.5 %all-gather.5.cloned.1.call-done = bf16[256,2048]{1,0:T(8,128)(2,1)} async-done(((bf16[64,2048]{1,0:T(8,128)(2,1)}), bf16[256,2048]{1,0:T(8,128)(2,1)}) %all-gather.5.cloned.1.call-update) | async-done | bytes 1048592 | tf_op jit(solution)/shard_map/all_gather | solution.py:23
  40.2 0.0 copy-start
  40.2 6.8 %convolution_multiply_fusion = f32[256,1792]{1,0:T(8,128)} fusion(bf16[256,2048]{1,0:T(8,128)(2,1)} %all-gather.5.cloned.1.call-done, bf16[2048,1792]{1,0:T(8,128)(2,1)} %param.7), kind=kOutput, calls=%fused_computation.5 | convolution fusion | flops 1879506944 | bytes 10223616 | tf_op jit(solution)/shard_map/dot_general | solution.py:28
  47.0 0.0 copy-done
  47.0 6.6 %convolution_multiply_fusion.1 = f32[256,1792]{1,0:T(8,128)} fusion(bf16[256,2048]{1,0:T(8,128)(2,1)S(1)} %copy-done, bf16[2048,1792]{1,0:T(8,128)(2,1)} %param.8), kind=kOutput, calls=%fused_computation.6 | convolution fusion | flops 1879506944 | bytes 10223616 | tf_op jit(solution)/shard_map/dot_general | solution.py:29
  53.6 15.6 %all-gather.3.cloned.1.call-done = bf16[256,2048]{1,0:T(8,128)(2,1)} async-done(((bf16[64,2048]{1,0:T(8,128)(2,1)}), bf16[256,2048]{1,0:T(8,128)(2,1)}) %all-gather.3.cloned.1.call-update) | async-done | bytes 1048592 | tf_op jit(solution)/shard_map/all_gather | solution.py:24
  69.3 7.1 %multiply_convert_fusion.4 = (bf16[256,1792]{1,0:T(8,128)(2,1)S(1)}, bf16[256,1792]{1,0:T(8,128)(2,1)S(1)}) fusion(f32[256,1792]{1,0:T(8,128)} %convolution_multiply_fusion, f32[256,1792]{1,0:T(8,128)} %convolution_multiply_fusion.1, bf16[256,2048]{1,0:T(8,128)(2,1)} %all-gather.3.cloned.1.call-done, bf16[1792,2048]{1,0:T(8,128)(2,1)} %param.9), kind=kOutput, calls=%fused_computation.11 | convolution fusion | flops 1885470720 | bytes 13893632 | tf_op jit(solution)/shard_map/dot_general | solution.py:11
  76.3 5.2 %fusion.6 = f32[256,2048]{1,0:T(8,128)S(1)} fusion(bf16[256,1792]{1,0:T(8,128)(2,1)S(1)} %get-tuple-element.9, bf16[2048,1792]{1,0:T(8,128)(2,1)} %param.7), kind=kOutput, calls=%fused_computation.16 | convolution fusion | flops 1879048192 | bytes 10354688 | tf_op jit(solution)/shard_map/dot_general | solution.py:11
  81.5 6.6 %fusion.2 = f32[256,2048]{1,0:T(8,128)} fusion(f32[256,2048]{1,0:T(8,128)S(1)} %fusion.6, bf16[256,1792]{1,0:T(8,128)(2,1)S(1)} %get-tuple-element.8, bf16[2048,1792]{1,0:T(8,128)(2,1)} %param.8), kind=kOutput, calls=%fused_computation.9 | convolution fusion | flops 1880096768 | bytes 12451840 | tf_op jit(solution)/shard_map/dot_general | solution.py:11
  88.1 0.0 reduce-scatter.2.cloned.1.call-update
  88.1 5.2 %fusion.1 = bf16[2048,1792]{0,1:T(8,128)(2,1)} fusion(bf16[256,1792]{1,0:T(8,128)(2,1)S(1)} %get-tuple-element.8, bf16[256,2048]{1,0:T(8,128)(2,1)S(1)} %copy-done), kind=kOutput, calls=%fused_computation.4 | convolution fusion | flops 1886388224 | bytes 9306112 | tf_op jit(solution)/shard_map/dot_general | solution.py:17
  93.2 10.1 %copy.10 = bf16[2048,1792]{1,0:T(8,128)(2,1)} copy(bf16[2048,1792]{0,1:T(8,128)(2,1)} %fusion.1) | data formatting | bytes 14680064
  103.3 5.1 %fusion = bf16[2048,1792]{0,1:T(8,128)(2,1)} fusion(bf16[256,1792]{1,0:T(8,128)(2,1)S(1)} %get-tuple-element.9, bf16[256,2048]{1,0:T(8,128)(2,1)S(1)} %copy-done), kind=kOutput, calls=%fused_computation.3 | convolution fusion | flops 1886388224 | bytes 9306112 | tf_op jit(solution)/shard_map/dot_general | solution.py:17
  108.5 10.1 %copy.9 = bf16[2048,1792]{1,0:T(8,128)(2,1)} copy(bf16[2048,1792]{0,1:T(8,128)(2,1)} %fusion) | data formatting | bytes 14680064
  118.6 0.0 copy-done.1
  118.6 0.0 copy-done.2
  118.6 6.8 %multiply_convert_fusion = bf16[1792,2048]{1,0:T(8,128)(2,1)} fusion(bf16[256,2048]{1,0:T(8,128)(2,1)S(1)} %copy-done.1, f32[256,1792]{1,0:T(8,128)} %convolution_multiply_fusion.1, f32[256,1792]{1,0:T(8,128)S(1)} %copy-done.2), kind=kOutput, calls=%fused_computation | convolution fusion | flops 1889140736 | bytes 12058624 | tf_op jit(solution)/shard_map/dot_general | solution.py:17
  125.4 6.2 %reduce-scatter.2.cloned.1.call-done = f32[64,2048]{1,0:T(8,128)} async-done(((f32[256,2048]{1,0:T(8,128)}), f32[64,2048]{1,0:T(8,128)}) %reduce-scatter.2.cloned.1.call-update) | async-done | bytes 524304 | tf_op jit(solution)/shard_map/reduce_scatter | solution.py:39
  131.6 1.8 %convert_element_type.29 = bf16[64,2048]{1,0:T(8,128)(2,1)} convert(f32[64,2048]{1,0:T(8,128)} %reduce-scatter.2.cloned.1.call-done) | non-fusion elementwise | flops 131072 | bytes 786432 | tf_op jit(solution)/shard_map/convert_element_type | solution.py:46
  (2 shorter events, 0.0 us)
Async XLA Ops:
  7.2 33.1 %all-gather.5.cloned.1.call-start = ((), (), s32[]{:S(2)}) async-start(), calls=%async_computation.2 | async-start | bytes 1310720 | tf_op jit(solution)/shard_map/all_gather | solution.py:23
  7.9 61.4 %all-gather.3.cloned.1.call-start = ((), (), s32[]{:S(2)}) async-start(), calls=%async_computation.1 | async-start | bytes 1310720 | tf_op jit(solution)/shard_map/all_gather | solution.py:24
  8.6 122.9 %reduce-scatter.2.cloned.1.call-start = ((), (), s32[]{:S(2)}) async-start(), calls=%async_computation.3 | async-start | bytes 2621440 | tf_op jit(solution)/shard_map/reduce_scatter | solution.py:39
  40.2 6.8 %copy-start = (bf16[256,2048]{1,0:T(8,128)(2,1)S(1)}, bf16[256,2048]{1,0:T(8,128)(2,1)}, u32[]{:S(2)}) copy-start(bf16[256,2048]{1,0:T(8,128)(2,1)} %all-gather.5.cloned.1.call-done) | copy-start | bytes 3145732
  108.5 10.1 %copy-start.1 = (bf16[256,2048]{1,0:T(8,128)(2,1)S(1)}, bf16[256,2048]{1,0:T(8,128)(2,1)}, u32[]{:S(2)}) copy-start(bf16[256,2048]{1,0:T(8,128)(2,1)} %all-gather.3.cloned.1.call-done) | copy-start | bytes 3145732
  108.5 10.1 %copy-start.2 = (f32[256,1792]{1,0:T(8,128)S(1)}, f32[256,1792]{1,0:T(8,128)}, u32[]{:S(2)}) copy-start(f32[256,1792]{1,0:T(8,128)} %convolution_multiply_fusion) | copy-start | bytes 5505028
Sparse Core Ops, SparseCore 0:
  9.6 30.6 all-gather.4
  41.8 27.4 all-gather.2
  88.2 43.3 reduce-scatter.1
where the time goes:
time: 141 us; the launch traced here: 140 us
  waiting for transfers between devices  54.7 us (39%)
  matrix products  49.3 us (35%)
  local copies, waits for them, and re-layouts  20.2 us (14%)
  between operations  13.8 us (10%)
  other arithmetic  1.77 us (1%)
    all_gather x1, waiting for transfers between devices, on_device(): tokens_all = lax.all_gather(inputs, 'tensor', axis=0, tiled=True)  31.5 us
    unnamed x8, local copies, waits for them, and re-layouts  20.2 us
    dot_general x3, matrix products, contract_last(): lax.dot_general(left, right, (((1,), (1,)), ((), ())), preferred_element_...  18.8 us
    dot_general x3, matrix products, contract_first(): lax.dot_general(left, right, (((0,), (0,)), ((), ())), preferred_element_...  17.1 us
    all_gather x1, waiting for transfers between devices, on_device(): grads_all = lax.all_gather(grad_out, 'tensor', axis=0, tiled=True)  15.6 us
    dot_general x1, matrix products, on_device(): jnp.dot(tokens_all, gate_weight, preferred_element_type=jnp.float32)  6.77 us
    dot_general x1, matrix products, on_device(): jnp.dot(tokens_all, up_weight, preferred_element_type=jnp.float32)  6.64 us
    reduce_scatter x1, waiting for transfers between devices, on_device(): lax.psum_scatter(contract_last(d_gate, gate_weight) * inv_hidden + contra...  6.19 us
  transfers between devices with their start and end apart: 3, of which 3 were waited for; matrix products, arithmetic and copies ran while one was open for 36% of the time, Pallas kernels for 0%

commit v1 on v0

v1 whole, which is shorter than its diff:
```python
import functools

import jax
import jax.numpy as jnp
from jax import lax
from jax.experimental import pallas as pl
from jax.experimental.pallas import tpu as pltpu
from jax.sharding import PartitionSpec as P

MESH = pl.DeviceIdType.MESH
BF16 = jnp.bfloat16
F32 = jnp.float32


def dot_nn(a, b):
    return jnp.dot(a, b, preferred_element_type=F32)


def dot_nt(a, b):
    return lax.dot_general(a, b, (((1,), (1,)), ((), ())), preferred_element_type=F32)


def tile_of(size):
    return 256 if size % 256 == 0 else size


def tiles(size, body):
    width = tile_of(size)
    count = size // width
    if count == 1:
        body(slice(None))
        return

    @pl.loop(0, count)
    def _(t):
        body(pl.ds(pl.multiple_of(t * width, width), width))


def forward_kernel(
    n, scales,
    x_in, g_in, wg_in, wu_in, wd_in,
    x_all, g_all, hidden, d_gate, d_up, part,
    wg, wu, wd, gate, up,
    local_sem, send_sem, recv_sem,
):
    inv_width, inv_hidden = scales
    me = lax.axis_index("tensor")
    has_left, has_right = me > 0, me < n - 1
    rows, width = x_in.shape
    units = wg.shape[1]
    full = (x_all, g_all)
    own = (x_in, g_in)

    loads = [
        pltpu.make_async_copy(source, target, local_sem.at[i])
        for i, (source, target) in enumerate(
            (
                (x_in, x_all.at[me]),
                (wg_in, wg),
                (wu_in, wu),
                (g_in, g_all.at[me]),
                (wd_in, wd),
            )
        )
    ]

    def send(kind, way, shard, source=None):
        return pltpu.make_async_remote_copy(
            src_ref=full[kind].at[shard] if source is None else source,
            dst_ref=full[kind].at[shard],
            send_sem=send_sem.at[kind, way, shard],
            recv_sem=recv_sem.at[kind, shard],
            device_id={"tensor": me - 1 if way == 0 else me + 1},
            device_id_type=MESH,
        )

    barrier = pltpu.get_barrier_semaphore()

    @pl.when(has_left)
    def _():
        pl.semaphore_signal(barrier, inc=1, device_id={"tensor": me - 1}, device_id_type=MESH)

    @pl.when(has_right)
    def _():
        pl.semaphore_signal(barrier, inc=1, device_id={"tensor": me + 1}, device_id_type=MESH)

    for load in loads:
        load.start()

    @pl.when(has_left & has_right)
    def _():
        pl.semaphore_wait(barrier, 2)

    @pl.when(has_left != has_right)
    def _():
        pl.semaphore_wait(barrier, 1)

    @pl.when(has_left)
    def _():
        send(0, 0, me, x_in).start()

    @pl.when(has_right)
    def _():
        send(0, 1, me, x_in).start()

    def arrive(kind, s):
        right, left = me + s, me - s

        @pl.when((s > 0) & (right < n))
        def _():
            send(kind, 0, right).wait_recv()

            @pl.when(has_left)
            def _():
                send(kind, 0, right).start()

        @pl.when((s > 0) & (left >= 0))
        def _():
            send(kind, 1, left).wait_recv()

            @pl.when(has_right)
            def _():
                send(kind, 1, left).start()

    def both(s, body):
        @pl.when(me + s < n)
        def _():
            body(me + s)

        @pl.when((s > 0) & (me - s >= 0))
        def _():
            body(me - s)

    def first_half(shard):
        def body(cols):
            gate[shard, :, cols] = dot_nn(x_all[shard], wg[:, cols]) * inv_width
            up[shard, :, cols] = dot_nn(x_all[shard], wu[:, cols]) * inv_width

        tiles(units, body)

    def second_half(shard):
        def body(cols):
            d_hidden = dot_nt(g_all[shard], wd[cols, :]) * inv_width
            a, b = gate[shard, :, cols], up[shard, :, cols]
            sig = 1.0 / (1.0 + jnp.exp(-a))
            act = a * sig
            hidden[shard, :, cols] = (act * b).astype(BF16)
            d_gate[shard, :, cols] = (d_hidden * b * sig * (1.0 + a * (1.0 - sig))).astype(BF16)
            d_up[shard, :, cols] = (d_hidden * act).astype(BF16)

        tiles(units, body)

    def x_step(s, carry):
        arrive(0, s)

        @pl.when(has_left & (me + s == n - 1))
        def _():
            send(1, 0, me, g_in).start()

        @pl.when(has_right & (me - s == 0))
        def _():
            send(1, 1, me, g_in).start()

        @pl.when(s == 0)
        def _():
            for load in loads[:3]:
                load.wait()

        both(s, first_half)
        return carry

    lax.fori_loop(0, n, x_step, 0)

    def g_step(s, carry):
        arrive(1, s)

        @pl.when(s == 0)
        def _():
            for load in loads[3:]:
                load.wait()

        both(s, second_half)
        return carry

    lax.fori_loop(0, n, g_step, 0)

    def grad_inputs_tile(cols):
        dg = d_gate[...].reshape(n * rows, units)
        du = d_up[...].reshape(n * rows, units)
        total = dot_nt(dg, wg[cols, :]) + dot_nt(du, wu[cols, :])
        part[:, :, cols] = (total * inv_hidden).astype(part.dtype).reshape(n, rows, total.shape[1])

    tiles(width, grad_inputs_tile)

    def drain(s, carry):
        for kind in range(2):
            @pl.when(has_left & (me + s < n))
            def _():
                send(kind, 0, me + s).wait_send()

            @pl.when(has_right & (me - s >= 0))
            def _():
                send(kind, 1, me - s).wait_send()

        return carry

    lax.fori_loop(0, n, drain, 0)


def weights_kernel(inv_rows, x, g, h, dg, du, gg, gu, gd, ht):
    @pl.when(pl.program_id(0) == 0)
    def _():
        ht[...] = h[...].T

    xt = x[...].T
    gg[...] = (dot_nn(xt, dg[...]) * inv_rows).astype(BF16)
    gu[...] = (dot_nn(xt, du[...]) * inv_rows).astype(BF16)
    gd[...] = (dot_nn(ht[...], g[...]) * inv_rows).astype(BF16)


def on_device(n, x, g, wg, wu, wd):
    rows, width = x.shape
    units = wg.shape[1]
    tokens = n * rows
    vmem = pl.BlockSpec(memory_space=pltpu.VMEM)
    anywhere = pl.BlockSpec(memory_space=pl.ANY)
    scales = (width ** -0.5, (2 * n * units) ** -0.5)
    shape = jax.ShapeDtypeStruct
    x_all, g_all, hidden, d_gate, d_up, part = pl.pallas_call(
        functools.partial(forward_kernel, n, scales),
        out_shape=(
            shape((n, rows, width), BF16),
            shape((n, rows, width), BF16),
            shape((n, rows, units), BF16),
            shape((n, rows, units), BF16),
            shape((n, rows, units), BF16),
            shape((n, rows, width), BF16),
        ),
        in_specs=[anywhere] * 5,
        out_specs=(vmem,) * 6,
        scratch_shapes=[
            pltpu.VMEM((width, units), BF16),
            pltpu.VMEM((width, units), BF16),
            pltpu.VMEM((units, width), BF16),
            pltpu.VMEM((n, rows, units), F32),
            pltpu.VMEM((n, rows, units), F32),
            pltpu.SemaphoreType.DMA((5,)),
            pltpu.SemaphoreType.DMA((2, 2, n)),
            pltpu.SemaphoreType.DMA((2, n)),
        ],
        compiler_params=pltpu.CompilerParams(
            collective_id=0, has_side_effects=True, vmem_limit_bytes=48 * 2**20
        ),
        name="gather_forward",
    )(x, g, wg, wu, wd)
    x_all, g_all, part = (a.reshape(tokens, width) for a in (x_all, g_all, part))
    hidden, d_gate, d_up = (a.reshape(tokens, units) for a in (hidden, d_gate, d_up))
    grad_inputs = lax.psum_scatter(part, "tensor", scatter_dimension=0, tiled=True)
    block = 256
    whole = lambda i: (0, 0)
    grads = pl.pallas_call(
        functools.partial(weights_kernel, tokens ** -0.5),
        grid=(width // block,),
        out_shape=(
            shape((width, units), BF16),
            shape((width, units), BF16),
            shape((units, width), BF16),
        ),
        in_specs=[
            pl.BlockSpec((tokens, block), lambda i: (0, i)),
            pl.BlockSpec((tokens, block), lambda i: (0, i)),
            pl.BlockSpec((tokens, units), whole),
            pl.BlockSpec((tokens, units), whole),
            pl.BlockSpec((tokens, units), whole),
        ],
        out_specs=(
            pl.BlockSpec((block, units), lambda i: (i, 0)),
            pl.BlockSpec((block, units), lambda i: (i, 0)),
            pl.BlockSpec((units, block), lambda i: (0, i)),
        ),
        scratch_shapes=[pltpu.VMEM((units, tokens), BF16)],
        compiler_params=pltpu.CompilerParams(vmem_limit_bytes=40 * 2**20),
        cost_estimate=pl.CostEstimate(
            flops=6 * tokens * width * units,
            bytes_accessed=6 * width * units + 10 * tokens * width,
            transcendentals=0,
        ),
        name="weight_grads",
    )(x_all, g_all, hidden, d_gate, d_up)
    return (grad_inputs, *grads)


def solution(mesh):
    placed = (
        P(("dp", "tensor"), None),
        P(("dp", "tensor"), None),
        P(None, "tensor"),
        P(None, "tensor"),
        P("tensor", None),
    )
    return jax.shard_map(
        functools.partial(on_device, mesh.shape["tensor"]),
        mesh=mesh,
        in_specs=placed,
        out_specs=(
            P(("dp", "tensor"), None),
            P("dp", "tensor"),
            P("dp", "tensor"),
            P(("dp", "tensor"), None),
        ),
        check_vma=False,
    )
```

time: 141 us -> 97 us (0.69)
  Pallas kernels: 0 us -> 62 us
  matrix products: 49.3 us -> 0 us
  waiting for transfers between devices: 54.7 us -> 14.6 us
  local copies, waits for them, and re-layouts: 20.2 us -> 6.08 us
  other arithmetic: 1.77 us -> 0 us
    pallas_call x0 -> x2, Pallas kernels: none -> 62 us  [the longest x1 51.9 us: on_device(): pl.pallas_call(functools.partial(forward_kernel, n, scales), out_shape=(s...]
    dot_general x8 -> x0, matrix products: 49.3 us -> none  [the longest x3 18.8 us: contract_last(): lax.dot_general(left, right, (((1,), (1,)), ((), ())), preferred_element_...]
    all_gather x2 -> x0, waiting for transfers between devices: 47.1 us -> none  [the longest x1 31.5 us: on_device(): tokens_all = lax.all_gather(inputs, 'tensor', axis=0, tiled=True)]
    unnamed x8 -> x12, local copies, waits for them, and re-layouts: 20.2 us -> 6.08 us
    reduce_scatter x1, waiting for transfers between devices: 6.19 us -> 14.6 us  [on_device(): lax.psum_scatter(part, 'tensor', scatter_dimension=0, tiled=True)]
    convert_element_type x1 -> x0, other arithmetic: 1.77 us -> none  [on_device(): grad_inputs = summed.astype(jnp.bfloat16)]
  transfers between devices with their start and end apart: 3 -> 1, of which waited for: 3 -> 1; matrix products, arithmetic and copies ran while one was open for 36% -> 0% of each run, Pallas kernels for 0% -> 10%
where the time goes in v1:
time: 97 us; the launch traced here: 96.8 us
  Pallas kernels  62 us (64%)
  waiting for transfers between devices  14.6 us (15%)
  between operations  14.1 us (15%)
  local copies, waits for them, and re-layouts  6.08 us (6%)
    pallas_call x1, Pallas kernels, on_device(): pl.pallas_call(functools.partial(forward_kernel, n, scales), out_shape=(s...  51.9 us
    reduce_scatter x1, waiting for transfers between devices, on_device(): lax.psum_scatter(part, 'tensor', scatter_dimension=0, tiled=True)  14.6 us
    pallas_call x1, Pallas kernels, on_device(): pl.pallas_call(functools.partial(weights_kernel, tokens ** (-0.5)), grid=...  10.1 us
    unnamed x12, local copies, waits for them, and re-layouts  6.08 us
  transfers between devices with their start and end apart: 1, of which 1 were waited for; matrix products, arithmetic and copies ran while one was open for 0% of the time, Pallas kernels for 10%

profile of v1, /device:TPU:0, one launch (start us, length us, event | category | flops | bytes accessed | tf_op | source)
XLA Modules:
  0.0 96.8 jit_solution(5619359061431503821)
XLA Ops:
  7.2 0.0 reduce-scatter.2.cloned.1.call-start
  7.2 0.0 copy-start
  7.2 0.9 copy-done
  8.2 0.0 copy-start.1
  8.2 0.9 copy-done.1
  9.1 51.9 %gather_forward.1 = (bf16[4,64,2048]{2,1,0:T(8,128)(2,1)S(1)}, bf16[4,64,2048]{2,1,0:T(8,128)(2,1)S(1)}, bf16[4,64,1792]{2,1,0:T(8,128)(2,1)S(1)}, bf16[4,64,179...) custom-call(bf16[64,2048]{1,0:T(8,128)(2,1)S(1)} %copy-done, ...), custom_call_target="tpu_custom_call" | custom-call | tf_op jit(solution)/shard_map/gather_forward/pallas_call | solution.py:229
  61.0 0.0 copy-start.2
  61.0 0.9 copy-done.2
  62.0 0.0 copy-start.4
  62.0 0.9 copy-done.4
  62.9 0.0 reduce-scatter.2.cloned.1.call-update
  62.9 0.0 copy-start.3
  62.9 1.2 %copy-done.3 = bf16[4,64,1792]{2,1,0:T(8,128)(2,1)S(1)} copy-done((bf16[4,64,1792]{2,1,0:T(8,128)(2,1)S(1)}, bf16[4,64,1792]{2,1,0:T(8,128)(2,1)}, u32[]{:S(2)}) %copy-start.3) | copy-done | bytes 917528
  64.1 0.0 copy-start.5
  64.1 1.2 %copy-done.5 = bf16[4,64,1792]{2,1,0:T(8,128)(2,1)S(1)} copy-done((bf16[4,64,1792]{2,1,0:T(8,128)(2,1)S(1)}, bf16[4,64,1792]{2,1,0:T(8,128)(2,1)}, u32[]{:S(2)}) %copy-start.5) | copy-done | bytes 917528
  65.3 10.1 %weight_grads.1 = (bf16[2048,1792]{1,0:T(8,128)(2,1)}, bf16[2048,1792]{1,0:T(8,128)(2,1)}, bf16[1792,2048]{1,0:T(8,128)(2,1)}) custom-call(bf16[256,2048]{1,0:T(8,128)(2,1)S(1)} %bitcast.6, bf16[256,2048]{1,0:T(8,128)(2,1)S(1)} %bitcast.7, bf16[256,1792]{1,0:T(8,128)(2,1)S(1)} %bitcast.8, bf16[256,1792]{1,0:T(8,128)(2,1)S(1)} %bitcast.9, ...), custom_call_target="tpu_custom_call" | custom-call | flops 5637144576 | bytes 27262976 | tf_op jit(solution)/shard_map/weight_grads/pallas_call | solution.py:261
  75.3 14.6 %reduce-scatter.2.cloned.1.call-done = bf16[64,2048]{1,0:T(8,128)(2,1)} async-done(((bf16[256,2048]{1,0:T(8,128)(2,1)}), bf16[64,2048]{1,0:T(8,128)(2,1)}) %reduce-scatter.2.cloned.1.call-update) | async-done | bytes 262160 | tf_op jit(solution)/shard_map/reduce_scatter | solution.py:258
Async XLA Ops:
  7.2 82.8 %reduce-scatter.2.cloned.1.call-start = ((), (), s32[]{:S(2)}) async-start(), calls=%async_computation.1 | async-start | bytes 1310720 | tf_op jit(solution)/shard_map/reduce_scatter | solution.py:258
  7.2 1.0 copy-start
  8.2 0.9 copy-start.1
  61.0 0.9 copy-start.2
  62.0 0.9 copy-start.4
  62.9 1.2 %copy-start.3 = (bf16[4,64,1792]{2,1,0:T(8,128)(2,1)S(1)}, bf16[4,64,1792]{2,1,0:T(8,128)(2,1)}, u32[]{:S(2)}) copy-start(bf16[4,64,1792]{2,1,0:T(8,128)(2,1)} %copy-done.2) | copy-start | bytes 2752516
  64.1 1.2 %copy-start.5 = (bf16[4,64,1792]{2,1,0:T(8,128)(2,1)S(1)}, bf16[4,64,1792]{2,1,0:T(8,128)(2,1)}, u32[]{:S(2)}) copy-start(bf16[4,64,1792]{2,1,0:T(8,128)(2,1)} %copy-done.4) | copy-start | bytes 2752516
Sparse Core Ops, SparseCore 0:
  63.0 26.8 reduce-scatter.1

commit v2 on v1

--- a/solution.py
+++ b/solution.py
@@ -39,17 +39,19 @@
 def forward_kernel(
     n, scales,
     x_in, g_in, wg_in, wu_in, wd_in,
-    x_all, g_all, hidden, d_gate, d_up, part,
-    wg, wu, wd, gate, up,
-    local_sem, send_sem, recv_sem,
+    out, x_all, g_all, hidden, d_gate, d_up,
+    wg, wu, wd, gate, up, part, stage, from_side,
+    local_sem, send_sem, recv_sem, sum_send, sum_recv,
 ):
     inv_width, inv_hidden = scales
     me = lax.axis_index("tensor")
-    has_left, has_right = me > 0, me < n - 1
-    rows, width = x_in.shape
+    last = n - 1
+    has_left, has_right = me > 0, me < last
     units = wg.shape[1]
+    chunks, chunk = part.shape[1], part.shape[3]
     full = (x_all, g_all)
-    own = (x_in, g_in)
+    exists = (has_left, has_right)
+    LEFT, RIGHT = 0, 1
 
     loads = [
         pltpu.make_async_copy(source, target, local_sem.at[i])
@@ -64,25 +66,34 @@
         )
     ]
 
+    def device(way):
+        return {"tensor": me - 1 if way == LEFT else me + 1}
+
     def send(kind, way, shard, source=None):
         return pltpu.make_async_remote_copy(
             src_ref=full[kind].at[shard] if source is None else source,
             dst_ref=full[kind].at[shard],
             send_sem=send_sem.at[kind, way, shard],
             recv_sem=recv_sem.at[kind, shard],
-            device_id={"tensor": me - 1 if way == 0 else me + 1},
+            device_id=device(way),
             device_id_type=MESH,
         )
 
+    def send_sum(way, shard, c):
+        return pltpu.make_async_remote_copy(
+            src_ref=stage.at[shard, c],
+            dst_ref=from_side.at[way, shard, c],
+            send_sem=sum_send.at[shard, c],
+            recv_sem=sum_recv.at[way, shard, c],
+            device_id=device(way),
+            device_id_type=MESH,
+        )
+
     barrier = pltpu.get_barrier_semaphore()
-
-    @pl.when(has_left)
-    def _():
-        pl.semaphore_signal(barrier, inc=1, device_id={"tensor": me - 1}, device_id_type=MESH)
-
-    @pl.when(has_right)
-    def _():
-        pl.semaphore_signal(barrier, inc=1, device_id={"tensor": me + 1}, device_id_type=MESH)
+    for way in (LEFT, RIGHT):
+        @pl.when(exists[way])
+        def _():
+            pl.semaphore_signal(barrier, inc=1, device_id=device(way), device_id_type=MESH)
 
     for load in loads:
         load.start()
@@ -95,41 +106,10 @@
     def _():
         pl.semaphore_wait(barrier, 1)
 
-    @pl.when(has_left)
-    def _():
-        send(0, 0, me, x_in).start()
-
-    @pl.when(has_right)
-    def _():
-        send(0, 1, me, x_in).start()
-
-    def arrive(kind, s):
-        right, left = me + s, me - s
-
-        @pl.when((s > 0) & (right < n))
+    for way in (LEFT, RIGHT):
+        @pl.when(exists[way])
         def _():
-            send(kind, 0, right).wait_recv()
-
-            @pl.when(has_left)
-            def _():
-                send(kind, 0, right).start()
-
-        @pl.when((s > 0) & (left >= 0))
-        def _():
-            send(kind, 1, left).wait_recv()
-
-            @pl.when(has_right)
-            def _():
-                send(kind, 1, left).start()
-
-    def both(s, body):
-        @pl.when(me + s < n)
-        def _():
-            body(me + s)
-
-        @pl.when((s > 0) & (me - s >= 0))
-        def _():
-            body(me - s)
+            send(0, way, me, x_in).start()
 
     def first_half(shard):
         def body(cols):
@@ -150,57 +130,112 @@
 
         tiles(units, body)
 
-    def x_step(s, carry):
-        arrive(0, s)
-
-        @pl.when(has_left & (me + s == n - 1))
-        def _():
-            send(1, 0, me, g_in).start()
-
-        @pl.when(has_right & (me - s == 0))
-        def _():
-            send(1, 1, me, g_in).start()
-
-        @pl.when(s == 0)
+        @pl.loop(0, chunks)
+        def _(c):
+            cols = pl.ds(pl.multiple_of(c * chunk, chunk), chunk)
+            total = dot_nt(d_gate[shard], wg[cols, :]) + dot_nt(d_up[shard], wu[cols, :])
+            total = total * inv_hidden
+            part[shard, c] = total
+
+            @pl.when((me == 0) & (shard > me))
+            def _():
+                stage[shard, c] = total.astype(BF16)
+                send_sum(RIGHT, shard, c).start()
+
+            @pl.when((me == last) & (shard < me))
+            def _():
+                stage[shard, c] = total.astype(BF16)
+                send_sum(LEFT, shard, c).start()
+
+    from_right, from_left = last - me, me
+
+    def tick(i, carry):
+        for way, ahead in ((LEFT, from_right), (RIGHT, from_left)):
+            @pl.when(exists[way] & (i == 2 * ahead))
+            def _():
+                send(1, way, me, g_in).start()
+
+        arrivals = []
+        for way, ahead in ((LEFT, from_right), (RIGHT, from_left)):
+            sign = 1 if way == LEFT else -1
+            for kind in range(2):
+                valid = i < ahead if kind == 0 else (i >= ahead) & (i < 2 * ahead)
+                distance = 1 + i if kind == 0 else 2 * ahead - i
+                shard = me + sign * distance
+                arrivals.append((kind, valid, shard))
+
+                @pl.when(valid)
+                def _():
+                    send(kind, way, shard).wait_recv()
+
+                    @pl.when(exists[way])
+                    def _():
+                        send(kind, way, shard).start()
+
+        @pl.when(i == 0)
         def _():
             for load in loads[:3]:
                 load.wait()
-
-        both(s, first_half)
-        return carry
-
-    lax.fori_loop(0, n, x_step, 0)
-
-    def g_step(s, carry):
-        arrive(1, s)
-
-        @pl.when(s == 0)
-        def _():
+            first_half(me)
             for load in loads[3:]:
                 load.wait()
 
-        both(s, second_half)
+        for kind, valid, shard in arrivals:
+            @pl.when(valid)
+            def _():
+                (first_half, second_half)[kind](shard)
+
+        @pl.when(i == last - 1)
+        def _():
+            second_half(me)
+
         return carry
 
-    lax.fori_loop(0, n, g_step, 0)
-
-    def grad_inputs_tile(cols):
-        dg = d_gate[...].reshape(n * rows, units)
-        du = d_up[...].reshape(n * rows, units)
-        total = dot_nt(dg, wg[cols, :]) + dot_nt(du, wu[cols, :])
-        part[:, :, cols] = (total * inv_hidden).astype(part.dtype).reshape(n, rows, total.shape[1])
-
-    tiles(width, grad_inputs_tile)
+    lax.fori_loop(0, 2 * last, tick, 0)
+
+    def relay(k, carry):
+        distance = last - k
+
+        @pl.loop(0, chunks)
+        def _(c):
+            for way in (LEFT, RIGHT):
+                shard = me - distance if way == LEFT else me + distance
+
+                @pl.when(has_left & has_right & (shard >= 0) & (shard <= last))
+                def _():
+                    send_sum(way, shard, c).wait_recv()
+                    stage[shard, c] = (part[shard, c] + from_side[way, shard, c].astype(F32)).astype(BF16)
+                    send_sum(way, shard, c).start()
+
+        return carry
+
+    lax.fori_loop(0, last, relay, 0)
+
+    @pl.loop(0, chunks)
+    def _(c):
+        for way in (LEFT, RIGHT):
+            @pl.when(exists[1 - way])
+            def _():
+                send_sum(way, me, c).wait_recv()
+                part[me, c] += from_side[way, me, c].astype(F32)
+
+        out[:, pl.ds(pl.multiple_of(c * chunk, chunk), chunk)] = part[me, c].astype(BF16)
 
     def drain(s, carry):
-        for kind in range(2):
-            @pl.when(has_left & (me + s < n))
-            def _():
-                send(kind, 0, me + s).wait_send()
-
-            @pl.when(has_right & (me - s >= 0))
-            def _():
-                send(kind, 1, me - s).wait_send()
+        for way in (LEFT, RIGHT):
+            shard = me + s if way == LEFT else me - s
+
+            @pl.when(exists[way] & (shard >= 0) & (shard <= last))
+            def _():
+                for kind in range(2):
+                    send(kind, way, shard).wait_send()
+
+            target = me - s if way == LEFT else me + s
+
+            @pl.when((s > 0) & (target >= 0) & (target <= last))
+            def _():
+                for c in range(chunks):
+                    send_sum(way, target, c).wait_send()
 
         return carry
 
@@ -226,15 +261,17 @@
     anywhere = pl.BlockSpec(memory_space=pl.ANY)
     scales = (width ** -0.5, (2 * n * units) ** -0.5)
     shape = jax.ShapeDtypeStruct
-    x_all, g_all, hidden, d_gate, d_up, part = pl.pallas_call(
+    chunks = 4
+    chunk = width // chunks
+    grad_inputs, x_all, g_all, hidden, d_gate, d_up = pl.pallas_call(
         functools.partial(forward_kernel, n, scales),
         out_shape=(
+            shape((rows, width), BF16),
             shape((n, rows, width), BF16),
             shape((n, rows, width), BF16),
             shape((n, rows, units), BF16),
             shape((n, rows, units), BF16),
             shape((n, rows, units), BF16),
-            shape((n, rows, width), BF16),
         ),
         in_specs=[anywhere] * 5,
         out_specs=(vmem,) * 6,
@@ -244,18 +281,22 @@
             pltpu.VMEM((units, width), BF16),
             pltpu.VMEM((n, rows, units), F32),
             pltpu.VMEM((n, rows, units), F32),
+            pltpu.VMEM((n, chunks, rows, chunk), F32),
+            pltpu.VMEM((n, chunks, rows, chunk), BF16),
+            pltpu.VMEM((2, n, chunks, rows, chunk), BF16),
             pltpu.SemaphoreType.DMA((5,)),
             pltpu.SemaphoreType.DMA((2, 2, n)),
             pltpu.SemaphoreType.DMA((2, n)),
+            pltpu.SemaphoreType.DMA((n, chunks)),
+            pltpu.SemaphoreType.DMA((2, n, chunks)),
         ],
         compiler_params=pltpu.CompilerParams(
-            collective_id=0, has_side_effects=True, vmem_limit_bytes=48 * 2**20
+            collective_id=0, has_side_effects=True, vmem_limit_bytes=60 * 2**20
         ),
         name="gather_forward",
     )(x, g, wg, wu, wd)
-    x_all, g_all, part = (a.reshape(tokens, width) for a in (x_all, g_all, part))
+    x_all, g_all = (a.reshape(tokens, width) for a in (x_all, g_all))
     hidden, d_gate, d_up = (a.reshape(tokens, units) for a in (hidden, d_gate, d_up))
-    grad_inputs = lax.psum_scatter(part, "tensor", scatter_dimension=0, tiled=True)
     block = 256
     whole = lambda i: (0, 0)
     grads = pl.pallas_call(
@@ -279,7 +320,7 @@
             pl.BlockSpec((units, block), lambda i: (0, i)),
         ),
         scratch_shapes=[pltpu.VMEM((units, tokens), BF16)],
-        compiler_params=pltpu.CompilerParams(vmem_limit_bytes=40 * 2**20),
+        compiler_params=pltpu.CompilerParams(vmem_limit_bytes=60 * 2**20),
         cost_estimate=pl.CostEstimate(
             flops=6 * tokens * width * units,
             bytes_accessed=6 * width * units + 10 * tokens * width,

time: 97 us -> 92.5 us (0.954)
  Pallas kernels: 62 us -> 90.9 us
  waiting for transfers between devices: 14.6 us -> 0 us
  between operations: 14.1 us -> 0.65 us
  local copies, waits for them, and re-layouts: 6.08 us -> 0.71 us
    pallas_call x1, Pallas kernels: 51.9 us -> 79 us  [on_device(): pl.pallas_call(functools.partial(forward_kernel, n, scales), out_shape=(s...]
    reduce_scatter x1 -> x0, waiting for transfers between devices: 14.6 us -> none  [on_device(): lax.psum_scatter(part, 'tensor', scatter_dimension=0, tiled=True)]
    unnamed x12 -> x3, local copies, waits for them, and re-layouts: 6.08 us -> 0.71 us
    pallas_call x1, Pallas kernels: 10.1 us -> 11.9 us  [on_device(): pl.pallas_call(functools.partial(weights_kernel, tokens ** (-0.5)), grid=...]
  transfers between devices with their start and end apart: 1 -> 0, of which waited for: 1 -> 0; matrix products, arithmetic and copies ran while one was open for 0% -> 0% of each run, Pallas kernels for 10% -> 0%
where the time goes in v2:
time: 92.5 us; the launch traced here: 92.2 us
  Pallas kernels  90.9 us (98%)
    pallas_call x1, Pallas kernels, on_device(): pl.pallas_call(functools.partial(forward_kernel, n, scales), out_shape=(s...  79 us
    pallas_call x1, Pallas kernels, on_device(): pl.pallas_call(functools.partial(weights_kernel, tokens ** (-0.5)), grid=...  11.9 us

profile of v2, /device:TPU:0, one launch (start us, length us, event | category | flops | bytes accessed | tf_op | source)
XLA Modules:
  0.0 92.2 jit_solution(570993104826735225)
XLA Ops:
  0.6 79.0 %gather_forward.1 = (bf16[64,2048]{1,0:T(8,128)(2,1)}, bf16[4,64,2048]{2,1,0:T(8,128)(2,1)}, bf16[4,64,2048]{2,1,0:T(8,128)(2,1)}, bf16[4,64,1792]{2,1,0:T(8,128...) custom-call(bf16[64,2048]{1,0:T(8,128)(2,1)} %x_in.1, bf16[64,2048]{1,0:T(8,128)(2,1)} %g_in.1, ...), custom_call_target="tpu_custom_call" | custom-call | tf_op jit(solution)/shard_map/gather_forward/pallas_call | solution.py:266
  79.6 0.0 copy-start
  79.6 11.9 %weight_grads.1 = (bf16[2048,1792]{1,0:T(8,128)(2,1)}, bf16[2048,1792]{1,0:T(8,128)(2,1)}, bf16[1792,2048]{1,0:T(8,128)(2,1)}) custom-call(bf16[256,2048]{1,0:T(8,128)(2,1)} %bitcast.5, bf16[256,2048]{1,0:T(8,128)(2,1)} %bitcast.6, bf16[256,1792]{1,0:T(8,128)(2,1)} %bitcast.7, bf16[256,1792]{1,0:T(8,128)(2,1)} %bitcast.8, bf16[256,1792]{1,0:T(8,128)(2,1)} %bitcast.9), custom_call_target="tpu_custom_call" | custom-call | flops 5637144576 | bytes 27262976 | tf_op jit(solution)/shard_map/weight_grads/pallas_call | solution.py:302
  91.5 0.0 copy-done
  91.5 0.7 copy.10
Async XLA Ops:
  79.6 11.9 %copy-start = (bf16[64,2048]{1,0:T(8,128)(2,1)S(1)}, bf16[64,2048]{1,0:T(8,128)(2,1)}, u32[]{:S(2)}) copy-start(bf16[64,2048]{1,0:T(8,128)(2,1)} %get-tuple-element.26) | copy-start | bytes 786436

commit v3 on v2

--- a/solution.py
+++ b/solution.py
@@ -21,7 +21,7 @@
 
 
 def tile_of(size):
-    return 256 if size % 256 == 0 else size
+    return 896 if size % 896 == 0 else size
 
 
 def tiles(size, body):
@@ -51,6 +51,7 @@
     chunks, chunk = part.shape[1], part.shape[3]
     full = (x_all, g_all)
     exists = (has_left, has_right)
+    from_right, from_left = last - me, me
     LEFT, RIGHT = 0, 1
 
     loads = [
@@ -111,43 +112,65 @@
         def _():
             send(0, way, me, x_in).start()
 
-    def first_half(shard):
+    rows = x_in.shape[0]
+
+    def merged(ref, pair):
+        block = ref[pl.ds(2 * pair, 2)]
+        return block.reshape(2 * rows, block.shape[2])
+
+    def first_half(pair):
+        two = pl.ds(2 * pair, 2)
+
         def body(cols):
-            gate[shard, :, cols] = dot_nn(x_all[shard], wg[:, cols]) * inv_width
-            up[shard, :, cols] = dot_nn(x_all[shard], wu[:, cols]) * inv_width
+            x = merged(x_all, pair)
+            a = dot_nn(x, wg[:, cols]) * inv_width
+            gate[two, :, cols] = a.reshape(2, rows, a.shape[1])
+            b = dot_nn(x, wu[:, cols]) * inv_width
+            up[two, :, cols] = b.reshape(2, rows, b.shape[1])
 
         tiles(units, body)
 
-    def second_half(shard):
+    def second_half(pair):
+        two = pl.ds(2 * pair, 2)
+
         def body(cols):
-            d_hidden = dot_nt(g_all[shard], wd[cols, :]) * inv_width
-            a, b = gate[shard, :, cols], up[shard, :, cols]
+            d_hidden = dot_nt(merged(g_all, pair), wd[cols, :]) * inv_width
+            d_hidden = d_hidden.reshape(2, rows, d_hidden.shape[1])
+            a, b = gate[two, :, cols], up[two, :, cols]
             sig = 1.0 / (1.0 + jnp.exp(-a))
             act = a * sig
-            hidden[shard, :, cols] = (act * b).astype(BF16)
-            d_gate[shard, :, cols] = (d_hidden * b * sig * (1.0 + a * (1.0 - sig))).astype(BF16)
-            d_up[shard, :, cols] = (d_hidden * act).astype(BF16)
+            hidden[two, :, cols] = (act * b).astype(BF16)
+            d_gate[two, :, cols] = (d_hidden * b * sig * (1.0 + a * (1.0 - sig))).astype(BF16)
+            d_up[two, :, cols] = (d_hidden * act).astype(BF16)
 
         tiles(units, body)
 
         @pl.loop(0, chunks)
         def _(c):
             cols = pl.ds(pl.multiple_of(c * chunk, chunk), chunk)
-            total = dot_nt(d_gate[shard], wg[cols, :]) + dot_nt(d_up[shard], wu[cols, :])
-            total = total * inv_hidden
-            part[shard, c] = total
-
-            @pl.when((me == 0) & (shard > me))
-            def _():
-                stage[shard, c] = total.astype(BF16)
-                send_sum(RIGHT, shard, c).start()
-
-            @pl.when((me == last) & (shard < me))
-            def _():
-                stage[shard, c] = total.astype(BF16)
-                send_sum(LEFT, shard, c).start()
-
-    from_right, from_left = last - me, me
+            total = dot_nt(merged(d_gate, pair), wg[cols, :]) + dot_nt(merged(d_up, pair), wu[cols, :])
+            total = (total * inv_hidden).reshape(2, rows, chunk)
+            for half in range(2):
+                shard = 2 * pair + half
+                part[shard, c] = total[half]
+
+                @pl.when((me == 0) & (shard > me))
+                def _():
+                    stage[shard, c] = total[half].astype(BF16)
+                    send_sum(RIGHT, shard, c).start()
+
+                @pl.when((me == last) & (shard < me))
+                def _():
+                    stage[shard, c] = total[half].astype(BF16)
+                    send_sum(LEFT, shard, c).start()
+
+    def x_tick(shard):
+        return jnp.maximum(jnp.abs(shard - me) - 1, 0)
+
+    def g_tick(shard):
+        apart = jnp.abs(shard - me)
+        whole = jnp.where(shard > me, from_right, from_left)
+        return jnp.where(apart == 0, 0, 2 * whole - apart)
 
     def tick(i, carry):
         for way, ahead in ((LEFT, from_right), (RIGHT, from_left)):
@@ -155,14 +178,12 @@
             def _():
                 send(1, way, me, g_in).start()
 
-        arrivals = []
         for way, ahead in ((LEFT, from_right), (RIGHT, from_left)):
             sign = 1 if way == LEFT else -1
             for kind in range(2):
                 valid = i < ahead if kind == 0 else (i >= ahead) & (i < 2 * ahead)
                 distance = 1 + i if kind == 0 else 2 * ahead - i
                 shard = me + sign * distance
-                arrivals.append((kind, valid, shard))
 
                 @pl.when(valid)
                 def _():
@@ -174,20 +195,15 @@
 
         @pl.when(i == 0)
         def _():
-            for load in loads[:3]:
+            for load in loads:
                 load.wait()
-            first_half(me)
-            for load in loads[3:]:
-                load.wait()
-
-        for kind, valid, shard in arrivals:
-            @pl.when(valid)
-            def _():
-                (first_half, second_half)[kind](shard)
-
-        @pl.when(i == last - 1)
-        def _():
-            second_half(me)
+
+        @pl.loop(0, n // 2)
+        def _(pair):
+            for ready, work in ((x_tick, first_half), (g_tick, second_half)):
+                @pl.when(i == jnp.maximum(ready(2 * pair), ready(2 * pair + 1)))
+                def _():
+                    work(pair)
 
         return carry
 

time: 92.5 us -> 79.4 us (0.86)
  Pallas kernels: 90.9 us -> 77.8 us
    pallas_call x1, Pallas kernels: 79 us -> 65.9 us  [on_device(): pl.pallas_call(functools.partial(forward_kernel, n, scales), out_shape=(s...]
where the time goes in v3:
time: 79.4 us; the launch traced here: 79.1 us
  Pallas kernels  77.8 us (98%)
    pallas_call x1, Pallas kernels, on_device(): pl.pallas_call(functools.partial(forward_kernel, n, scales), out_shape=(s...  65.9 us
    pallas_call x1, Pallas kernels, on_device(): pl.pallas_call(functools.partial(weights_kernel, tokens ** (-0.5)), grid=...  11.9 us

profile of v3, /device:TPU:0, one launch (start us, length us, event | category | flops | bytes accessed | tf_op | source)
XLA Modules:
  0.0 79.1 jit_solution(11915761689734840752)
XLA Ops:
  0.6 65.9 %gather_forward.1 = (bf16[64,2048]{1,0:T(8,128)(2,1)}, bf16[4,64,2048]{2,1,0:T(8,128)(2,1)}, bf16[4,64,2048]{2,1,0:T(8,128)(2,1)}, bf16[4,64,1792]{2,1,0:T(8,128...) custom-call(bf16[64,2048]{1,0:T(8,128)(2,1)} %x_in.1, bf16[64,2048]{1,0:T(8,128)(2,1)} %g_in.1, ...), custom_call_target="tpu_custom_call" | custom-call | tf_op jit(solution)/shard_map/gather_forward/pallas_call | solution.py:282
  66.5 0.0 copy-start
  66.5 11.9 %weight_grads.1 = (bf16[2048,1792]{1,0:T(8,128)(2,1)}, bf16[2048,1792]{1,0:T(8,128)(2,1)}, bf16[1792,2048]{1,0:T(8,128)(2,1)}) custom-call(bf16[256,2048]{1,0:T(8,128)(2,1)} %bitcast.5, bf16[256,2048]{1,0:T(8,128)(2,1)} %bitcast.6, bf16[256,1792]{1,0:T(8,128)(2,1)} %bitcast.7, bf16[256,1792]{1,0:T(8,128)(2,1)} %bitcast.8, bf16[256,1792]{1,0:T(8,128)(2,1)} %bitcast.9), custom_call_target="tpu_custom_call" | custom-call | flops 5637144576 | bytes 27262976 | tf_op jit(solution)/shard_map/weight_grads/pallas_call | solution.py:318
  78.4 0.0 copy-done
  78.4 0.7 copy.10
Async XLA Ops:
  66.5 11.9 %copy-start = (bf16[64,2048]{1,0:T(8,128)(2,1)S(1)}, bf16[64,2048]{1,0:T(8,128)(2,1)}, u32[]{:S(2)}) copy-start(bf16[64,2048]{1,0:T(8,128)(2,1)} %get-tuple-element.26) | copy-start | bytes 786436

commit v4 on v3

--- a/solution.py
+++ b/solution.py
@@ -40,13 +40,15 @@
     n, scales,
     x_in, g_in, wg_in, wu_in, wd_in,
     out, x_all, g_all, hidden, d_gate, d_up,
-    wg, wu, wd, gate, up, part, stage, from_side,
+    wg, wu, wd, wu_t, wd_t, gate, up, part, stage, from_side,
     local_sem, send_sem, recv_sem, sum_send, sum_recv,
 ):
     inv_width, inv_hidden = scales
     me = lax.axis_index("tensor")
     last = n - 1
     has_left, has_right = me > 0, me < last
+    is_end = (me == 0) | (me == last)
+    wg_t = wd
     units = wg.shape[1]
     chunks, chunk = part.shape[1], part.shape[3]
     full = (x_all, g_all)
@@ -114,15 +116,15 @@
 
     rows = x_in.shape[0]
 
-    def merged(ref, pair):
-        block = ref[pl.ds(2 * pair, 2)]
-        return block.reshape(2 * rows, block.shape[2])
+    def merged(ref, first, count):
+        block = ref[pl.ds(first, count)]
+        return block.reshape(count * rows, block.shape[2])
 
     def first_half(pair):
         two = pl.ds(2 * pair, 2)
 
         def body(cols):
-            x = merged(x_all, pair)
+            x = merged(x_all, 2 * pair, 2)
             a = dot_nn(x, wg[:, cols]) * inv_width
             gate[two, :, cols] = a.reshape(2, rows, a.shape[1])
             b = dot_nn(x, wu[:, cols]) * inv_width
@@ -130,38 +132,53 @@
 
         tiles(units, body)
 
-    def second_half(pair):
-        two = pl.ds(2 * pair, 2)
+    def flip(source, target):
+        block = 256 if source.shape[0] % 256 == 0 else source.shape[0]
+
+        @pl.loop(0, source.shape[0] // block)
+        def _(r):
+            at = pl.ds(pl.multiple_of(r * block, block), block)
+            target[:, at] = source[at, :].T
+
+    def second_half(first, count, flipped):
+        group = pl.ds(first, count)
 
         def body(cols):
-            d_hidden = dot_nt(merged(g_all, pair), wd[cols, :]) * inv_width
-            d_hidden = d_hidden.reshape(2, rows, d_hidden.shape[1])
-            a, b = gate[two, :, cols], up[two, :, cols]
+            grads = merged(g_all, first, count)
+            d_hidden = (dot_nn(grads, wd_t[:, cols]) if flipped else dot_nt(grads, wd[cols, :])) * inv_width
+            d_hidden = d_hidden.reshape(count, rows, d_hidden.shape[1])
+            a, b = gate[group, :, cols], up[group, :, cols]
             sig = 1.0 / (1.0 + jnp.exp(-a))
             act = a * sig
-            hidden[two, :, cols] = (act * b).astype(BF16)
-            d_gate[two, :, cols] = (d_hidden * b * sig * (1.0 + a * (1.0 - sig))).astype(BF16)
-            d_up[two, :, cols] = (d_hidden * act).astype(BF16)
+            hidden[group, :, cols] = (act * b).astype(BF16)
+            d_gate[group, :, cols] = (d_hidden * b * sig * (1.0 + a * (1.0 - sig))).astype(BF16)
+            d_up[group, :, cols] = (d_hidden * act).astype(BF16)
 
         tiles(units, body)
 
         @pl.loop(0, chunks)
         def _(c):
             cols = pl.ds(pl.multiple_of(c * chunk, chunk), chunk)
-            total = dot_nt(merged(d_gate, pair), wg[cols, :]) + dot_nt(merged(d_up, pair), wu[cols, :])
-            total = (total * inv_hidden).reshape(2, rows, chunk)
-            for half in range(2):
-                shard = 2 * pair + half
-                part[shard, c] = total[half]
+            dg, du = merged(d_gate, first, count), merged(d_up, first, count)
+            if flipped:
+                total = dot_nn(dg, wg_t[:, cols]) + dot_nn(du, wu_t[:, cols])
+            else:
+                total = dot_nt(dg, wg[cols, :]) + dot_nt(du, wu[cols, :])
+            total = (total * inv_hidden).reshape(count, rows, chunk)
+            for at in range(count):
+                shard = first + at
+                part[shard, c] = total[at]
+                if not flipped:
+                    continue
 
                 @pl.when((me == 0) & (shard > me))
                 def _():
-                    stage[shard, c] = total[half].astype(BF16)
+                    stage[shard, c] = total[at].astype(BF16)
                     send_sum(RIGHT, shard, c).start()
 
                 @pl.when((me == last) & (shard < me))
                 def _():
-                    stage[shard, c] = total[half].astype(BF16)
+                    stage[shard, c] = total[at].astype(BF16)
                     send_sum(LEFT, shard, c).start()
 
     def x_tick(shard):
@@ -195,15 +212,35 @@
 
         @pl.when(i == 0)
         def _():
-            for load in loads:
+            for load in loads[:3]:
+                load.wait()
+
+        @pl.when(i == 1)
+        def _():
+            for load in loads[3:]:
                 load.wait()
 
         @pl.loop(0, n // 2)
         def _(pair):
-            for ready, work in ((x_tick, first_half), (g_tick, second_half)):
-                @pl.when(i == jnp.maximum(ready(2 * pair), ready(2 * pair + 1)))
-                def _():
-                    work(pair)
+            @pl.when(i == jnp.maximum(x_tick(2 * pair), x_tick(2 * pair + 1)))
+            def _():
+                first_half(pair)
+
+        @pl.when(is_end & (i == 1))
+        def _():
+            flip(wd, wd_t)
+            flip(wg, wg_t)
+            flip(wu, wu_t)
+
+        @pl.loop(0, n // 2)
+        def _(pair):
+            @pl.when(is_end & (i == jnp.maximum(g_tick(2 * pair), g_tick(2 * pair + 1))))
+            def _():
+                second_half(2 * pair, 2, True)
+
+        @pl.when(jnp.logical_not(is_end) & (i == 2 * jnp.maximum(from_right, from_left) - 1))
+        def _():
+            second_half(0, n, False)
 
         return carry
 
@@ -295,6 +332,8 @@
             pltpu.VMEM((width, units), BF16),
             pltpu.VMEM((width, units), BF16),
             pltpu.VMEM((units, width), BF16),
+            pltpu.VMEM((units, width), BF16),
+            pltpu.VMEM((width, units), BF16),
             pltpu.VMEM((n, rows, units), F32),
             pltpu.VMEM((n, rows, units), F32),
             pltpu.VMEM((n, chunks, rows, chunk), F32),

time: 79.4 us -> 74.4 us (0.937)
  Pallas kernels: 77.8 us -> 72.8 us
    pallas_call x1, Pallas kernels: 65.9 us -> 60.9 us  [on_device(): pl.pallas_call(functools.partial(forward_kernel, n, scales), out_shape=(s...]
where the time goes in v4:
time: 74.4 us; the launch traced here: 74.1 us
  Pallas kernels  72.8 us (98%)
    pallas_call x1, Pallas kernels, on_device(): pl.pallas_call(functools.partial(forward_kernel, n, scales), out_shape=(s...  60.9 us
    pallas_call x1, Pallas kernels, on_device(): pl.pallas_call(functools.partial(weights_kernel, tokens ** (-0.5)), grid=...  11.9 us

profile of v4, /device:TPU:0, one launch (start us, length us, event | category | flops | bytes accessed | tf_op | source)
XLA Modules:
  0.0 74.1 jit_solution(10642680152287554366)
XLA Ops:
  0.6 60.9 %gather_forward.1 = (bf16[64,2048]{1,0:T(8,128)(2,1)}, bf16[4,64,2048]{2,1,0:T(8,128)(2,1)}, bf16[4,64,2048]{2,1,0:T(8,128)(2,1)}, bf16[4,64,1792]{2,1,0:T(8,128...) custom-call(bf16[64,2048]{1,0:T(8,128)(2,1)} %x_in.1, bf16[64,2048]{1,0:T(8,128)(2,1)} %g_in.1, ...), custom_call_target="tpu_custom_call" | custom-call | tf_op jit(solution)/shard_map/gather_forward/pallas_call | solution.py:319
  61.6 0.0 copy-start
  61.6 11.9 %weight_grads.1 = (bf16[2048,1792]{1,0:T(8,128)(2,1)}, bf16[2048,1792]{1,0:T(8,128)(2,1)}, bf16[1792,2048]{1,0:T(8,128)(2,1)}) custom-call(bf16[256,2048]{1,0:T(8,128)(2,1)} %bitcast.5, bf16[256,2048]{1,0:T(8,128)(2,1)} %bitcast.6, bf16[256,1792]{1,0:T(8,128)(2,1)} %bitcast.7, bf16[256,1792]{1,0:T(8,128)(2,1)} %bitcast.8, bf16[256,1792]{1,0:T(8,128)(2,1)} %bitcast.9), custom_call_target="tpu_custom_call" | custom-call | flops 5637144576 | bytes 27262976 | tf_op jit(solution)/shard_map/weight_grads/pallas_call | solution.py:357
  73.4 0.0 copy-done
  73.4 0.7 copy.10
Async XLA Ops:
  61.6 11.9 %copy-start = (bf16[64,2048]{1,0:T(8,128)(2,1)S(1)}, bf16[64,2048]{1,0:T(8,128)(2,1)}, u32[]{:S(2)}) copy-start(bf16[64,2048]{1,0:T(8,128)(2,1)} %get-tuple-element.26) | copy-start | bytes 786436

commit v5 on v4

--- a/solution.py
+++ b/solution.py
@@ -352,7 +352,7 @@
     )(x, g, wg, wu, wd)
     x_all, g_all = (a.reshape(tokens, width) for a in (x_all, g_all))
     hidden, d_gate, d_up = (a.reshape(tokens, units) for a in (hidden, d_gate, d_up))
-    block = 256
+    block = 512
     whole = lambda i: (0, 0)
     grads = pl.pallas_call(
         functools.partial(weights_kernel, tokens ** -0.5),

time: 74.4 us -> 72.9 us (0.980)
  Pallas kernels: 72.8 us -> 71.4 us
    pallas_call x1, Pallas kernels: 11.9 us -> 10.4 us  [on_device(): pl.pallas_call(functools.partial(weights_kernel, tokens ** (-0.5)), grid=...]
where the time goes in v5:
time: 72.9 us; the launch traced here: 72.7 us
  Pallas kernels  71.4 us (98%)
    pallas_call x1, Pallas kernels, on_device(): pl.pallas_call(functools.partial(forward_kernel, n, scales), out_shape=(s...  60.9 us
    pallas_call x1, Pallas kernels, on_device(): pl.pallas_call(functools.partial(weights_kernel, tokens ** (-0.5)), grid=...  10.4 us

profile of v5, /device:TPU:0, one launch (start us, length us, event | category | flops | bytes accessed | tf_op | source)
XLA Modules:
  0.0 72.7 jit_solution(14134058737274216143)
XLA Ops:
  0.6 60.9 %gather_forward.1 = (bf16[64,2048]{1,0:T(8,128)(2,1)}, bf16[4,64,2048]{2,1,0:T(8,128)(2,1)}, bf16[4,64,2048]{2,1,0:T(8,128)(2,1)}, bf16[4,64,1792]{2,1,0:T(8,128...) custom-call(bf16[64,2048]{1,0:T(8,128)(2,1)} %x_in.1, bf16[64,2048]{1,0:T(8,128)(2,1)} %g_in.1, ...), custom_call_target="tpu_custom_call" | custom-call | tf_op jit(solution)/shard_map/gather_forward/pallas_call | solution.py:319
  61.6 0.0 copy-start
  61.6 10.4 %weight_grads.1 = (bf16[2048,1792]{1,0:T(8,128)(2,1)}, bf16[2048,1792]{1,0:T(8,128)(2,1)}, bf16[1792,2048]{1,0:T(8,128)(2,1)}) custom-call(bf16[256,2048]{1,0:T(8,128)(2,1)} %bitcast.5, bf16[256,2048]{1,0:T(8,128)(2,1)} %bitcast.6, bf16[256,1792]{1,0:T(8,128)(2,1)} %bitcast.7, bf16[256,1792]{1,0:T(8,128)(2,1)} %bitcast.8, bf16[256,1792]{1,0:T(8,128)(2,1)} %bitcast.9), custom_call_target="tpu_custom_call" | custom-call | flops 5637144576 | bytes 27262976 | tf_op jit(solution)/shard_map/weight_grads/pallas_call | solution.py:357
  72.0 0.0 copy-done
  72.0 0.7 copy.10
Async XLA Ops:
  61.6 10.5 %copy-start = (bf16[64,2048]{1,0:T(8,128)(2,1)S(1)}, bf16[64,2048]{1,0:T(8,128)(2,1)}, u32[]{:S(2)}) copy-start(bf16[64,2048]{1,0:T(8,128)(2,1)} %get-tuple-element.26) | copy-start | bytes 786436
